TPU v7x, 32 devices: a whole 2x2x4 slice. The times are simulated.
32 devices in a mesh: seq: 8 (over y, x, core), fsdp: 4 (over z).
Axes of the slice: x: 2, y: 2, z: 4, core: 2. Of those that a mesh axis runs over, the one named last changes fastest.
Arguments:
- hidden: bfloat16 [8192, 3584], P(('seq', 'fsdp')), may hold values from -6 to 6
- queries: bfloat16 [8192, 2048], P(('seq', 'fsdp')), may hold values from -360 to 360
- kv_weights: bfloat16 [2, 3584, 1024], P(None, 'fsdp'), may hold values from -0.09375 to 0.09375
- image_groups: int32 [8], P('seq'), may hold values 0 or 1
- doc_ids: int32 [8192], replicated, may hold values from 0 to 7, never falling along the last dimension, each value on 1 to 3072 neighbouring positions
Outputs:
- attended: bfloat16 [8192, 2048], P(('seq', 'fsdp'))
Inputs may be any that keep to these rules, and one draw needn't show every extreme that they name: `image_groups`: 1 marks a group of image tokens. `doc_ids`: never falling along the tokens; every document has 1 to 3072 tokens and one has exactly that many.
All inputs are finite; a program needn't handle non-finite values.
Results may differ from a plain program's by a relative error of at most 0.0055.
The roundings to bfloat16 on the way count: a program that leaves them out, or rounds other values in their place, can miss the bound.
Values may be sent and summed in bfloat16 or wider, within the bound.
A program may use at most 128 MiB of HBM per device.

v0:
```python
import math

import jax
import jax.numpy as jnp
from jax import lax
from jax.sharding import PartitionSpec as P

KVH = 4
HD = 128
QH = 16
SPAN = 3


def from_behind(block, axis, distance):
    devices = range(lax.axis_size(axis))
    route = [(i - distance, i) for i in devices if i - distance in devices]
    return lax.ppermute(block, axis, route)


def build_mask(query_pos, key_pos, doc_ids, is_image, own_start):
    key_doc = jnp.where(key_pos >= 0, doc_ids[jnp.maximum(key_pos, 0)], -1)
    query_doc = doc_ids[query_pos]
    same_doc = query_doc[:, None] == key_doc[None, :]
    earlier = key_pos[None, :] <= query_pos[:, None]
    own_image = jnp.logical_and(is_image, key_pos[None, :] >= own_start)
    return jnp.logical_and(same_doc, jnp.logical_or(earlier, own_image))


def attend(query_rows, keys_values, allowed):
    n_query = query_rows.shape[0]
    n_keys = keys_values.shape[0]
    per_group = QH // KVH
    score_scale = 1.0 / math.sqrt(HD)
    query_heads = query_rows.reshape(n_query, KVH, per_group, HD).transpose(1, 0, 2, 3)
    key_heads = keys_values[:, : KVH * HD].reshape(n_keys, KVH, HD).transpose(1, 0, 2)
    value_heads = keys_values[:, KVH * HD :].reshape(n_keys, KVH, HD).transpose(1, 0, 2)

    def one_head(operands):
        head_q, head_k, head_v = operands
        scores = (
            jnp.einsum("rgd,kd->grk", head_q, head_k, preferred_element_type=jnp.float32)
            * score_scale
        )
        scores = jnp.where(allowed[None], scores, -1e30)
        highest = jnp.max(scores, axis=-1, keepdims=True)
        weights = jnp.where(allowed[None], jnp.exp(scores - highest), 0.0)
        totals = jnp.sum(weights, axis=-1)
        summed = jnp.einsum(
            "grk,kd->rgd", weights.astype(jnp.bfloat16), head_v, preferred_element_type=jnp.float32
        )
        return (summed / jnp.transpose(totals)[:, :, None]).astype(jnp.bfloat16)

    mixed = lax.map(one_head, (query_heads, key_heads, value_heads))
    return mixed.transpose(1, 0, 2, 3).reshape(n_query, QH * HD)


def local(hidden, queries, kv_weights, image_groups, doc_ids):
    local_rows = hidden.shape[0]
    fsdp_count = lax.axis_size("fsdp")
    block_rows = local_rows * fsdp_count
    seq_place = lax.axis_index("seq")
    fsdp_place = lax.axis_index("fsdp")
    modality = image_groups[0]
    own_weight = lax.dynamic_index_in_dim(kv_weights, modality, 0, keepdims=False)
    own_kv = jnp.dot(
        hidden,
        lax.all_gather(own_weight, "fsdp", axis=0, tiled=True),
        preferred_element_type=jnp.float32,
    ).astype(jnp.bfloat16)
    block_kv = lax.all_gather(own_kv, "fsdp", axis=0, tiled=True)
    pieces = [block_kv]
    for offset in range(1, SPAN + 1):
        pieces.append(from_behind(block_kv, "seq", offset))
    window = jnp.concatenate(pieces, 0)
    block_index = jnp.arange(SPAN + 1, dtype=jnp.int32)
    key_pos = (
        (seq_place - block_index)[:, None] * block_rows
        + jnp.arange(block_rows, dtype=jnp.int32)[None, :]
    ).reshape(-1)
    query_pos = (seq_place * fsdp_count + fsdp_place) * local_rows + jnp.arange(
        local_rows, dtype=jnp.int32
    )
    allowed = build_mask(query_pos, key_pos, doc_ids, modality == 1, seq_place * block_rows)
    return attend(queries, window, allowed)


def solution(mesh):
    in_specs = (
        P(("seq", "fsdp"), None),
        P(("seq", "fsdp"), None),
        P(None, "fsdp", None),
        P("seq"),
        P(),
    )
    out_specs = P(("seq", "fsdp"), None)
    return jax.shard_map(local, mesh=mesh, in_specs=in_specs, out_specs=out_specs, check_vma=False)
```

profile of v0, /device:TPU:4, one launch (start us, length us, event | category | flops | bytes accessed | tf_op | source)
XLA Modules:
  0.0 417.0 jit_solution(9696746824338678360)
XLA Ops:
  7.3 2.9 constant_dynamic-slice_fusion
  10.4 133.8 %all-gather.6.cloned.1.call-done = bf16[1,3584,1024]{2,1,0:T(8,128)(2,1)} async-done(((bf16[1,896,1024]{2,1,0:T(8,128)(2,1)}), bf16[1,3584,1024]{2,1,0:T(8,128)(2,1)}) %all-gather.6.cloned.1.call-update) | async-done | bytes 7340048 | tf_op jit(solution)/shard_map/all_gather | solution.py:67
  144.1 6.0 %fusion.59 = bf16[256,1024]{0,1:T(8,128)(2,1)} fusion(bf16[256,3584]{1,0:T(8,128)(2,1)S(1)} %copy-done, bf16[1,3584,1024]{2,1,0:T(8,128)(2,1)} %all-gather.6.cloned.1.call-done), kind=kOutput, calls=%fused_computation.38 | convolution fusion | flops 1879310336 | bytes 9699328 | tf_op jit(solution)/shard_map/dot_general | solution.py:65
  150.1 44.6 %all-gather.4.cloned.1.call-done = bf16[1024,1024]{0,1:T(8,128)(2,1)} async-done(((bf16[256,1024]{0,1:T(8,128)(2,1)}), bf16[1024,1024]{0,1:T(8,128)(2,1)}) %all-gather.4.cloned.1.call-update) | async-done | bytes 2097168 | tf_op jit(solution)/shard_map/all_gather | solution.py:70
  196.6 3.4 collective-permute-start.1
  202.1 23.0 %gather_fusion.1 = s32[4096]{0:T(1024)S(1)} fusion(s32[8192]{0:T(1024)S(1)} %copy-done.1, s32[4096]{0:T(1024)S(1)} %bitcast_clamp_fusion), kind=kCustom, calls=%fused_computation.1 | custom fusion | bytes 49152 | tf_op jit(solution)/shard_map/gather | solution.py:21
  230.1 13.3 %collective-permute-done = bf16[1024,1024]{0,1:T(8,128)(2,1)} collective-permute-done((bf16[1024,1024]{0,1:T(8,128)(2,1)}, bf16[1024,1024]{0,1:T(8,128)(2,1)}, u32[]{:S(2)}, u32[]{:S(2)}) %collective-permute-start) | collective-permute-done | bytes 2097184 | tf_op jit(solution)/shard_map/ppermute | solution.py:17
  245.2 3.2 collective-permute-done.1
  250.2 63.0 %collective-permute-done.2 = bf16[1024,1024]{0,1:T(8,128)(2,1)} collective-permute-done((bf16[1024,1024]{0,1:T(8,128)(2,1)}, bf16[1024,1024]{0,1:T(8,128)(2,1)}, u32[]{:S(2)}, u32[]{:S(2)}) %collective-permute-start.2) | collective-permute-done | bytes 2097184 | tf_op jit(solution)/shard_map/ppermute | solution.py:17
  315.0 3.8 fusion.72
  318.7 6.4 %copy.10 = bf16[4096,4,128]{2,0,1:T(8,128)(2,1)} copy(bf16[4096,4,128]{0,2,1:T(8,128)(2,1)} %bitcast.113) | data formatting | bytes 8388608 | tf_op jit(solution)/shard_map/reshape | solution.py:35
  325.1 82.8 %while.11 = (s32[]{:T(128)}, bf16[4,256,4,128]{1,3,2,0:T(8,128)(2,1)}, bf16[4,4096,128]{1,2,0:T(8,128)(2,1)}, bf16[4,4096,128]{2,1,0:T(8,128)(2,1)}, bf16[4,256,...) while((s32[]{:T(128)}, ...), condition=%wide.region_3.4_spmd.clone, body=%wide.region_0.3_spmd.clone.sunk | while | flops 2177110016 | bytes 22593644 | solution.py:53
  325.1 3.4 or_and_fusion.2
  328.6 11.6 %fusion.85 = (f32[4,256]{1,0:T(4,128)S(1)}, bf16[4,256,4096]{1,2,0:T(8,128)(2,1)}) fusion(pred[256,4096]{0,1:T(8,128)(4,1)S(1)} %or_and_fusion.2, bf16[4,4096,128]{2,1,0:T(8,128)(2,1)} %get-tuple-element.193, s32[]{:T(128)} %get-tuple-element.179, bf16[4,256,4,128]{1,3,2,0:T(8,128)(2,1)} %get-tuple-element.194), kind=kOutput, calls=%fused_computation.55.clone.1 | convolution fusion | flops 1098911744 | bytes 11801600 | tf_op jit(solution)/shard_map/while/body/eval_jaxpr/sub | solution.py:46
  340.1 5.7 %fusion.86 = bf16[4,256,4,128]{1,3,2,0:T(8,128)(2,1)} fusion(bf16[4,256,4,128]{1,3,2,0:T(8,128)(2,1)} %get-tuple-element.180, s32[]{:T(128)} %get-tuple-element.179, bf16[4,256,4096]{1,2,0:T(8,128)(2,1)} %get-tuple-element.166, bf16[4,4096,128]{1,2,0:T(8,128)(2,1)} %get-tuple-element.192, f32[256,4]{0,1:T(4,128)S(1)} %bitcast.120), kind=kOutput, calls=%fused_computation.18.clone.1 | convolution fusion | flops 1074003968 | bytes 9704448 | tf_op jit(solution)/shard_map/while/body/eval_jaxpr/grk,kd->rgd/dot_general | solution.py:48
  345.8 3.4 or_and_fusion.2
  349.3 11.6 %fusion.85 = (f32[4,256]{1,0:T(4,128)S(1)}, bf16[4,256,4096]{1,2,0:T(8,128)(2,1)}) fusion(pred[256,4096]{0,1:T(8,128)(4,1)S(1)} %or_and_fusion.2, bf16[4,4096,128]{2,1,0:T(8,128)(2,1)} %get-tuple-element.193, s32[]{:T(128)} %get-tuple-element.179, bf16[4,256,4,128]{1,3,2,0:T(8,128)(2,1)} %get-tuple-element.194), kind=kOutput, calls=%fused_computation.55.clone.1 | convolution fusion | flops 1098911744 | bytes 11801600 | tf_op jit(solution)/shard_map/while/body/eval_jaxpr/sub | solution.py:46
  360.8 5.7 %fusion.86 = bf16[4,256,4,128]{1,3,2,0:T(8,128)(2,1)} fusion(bf16[4,256,4,128]{1,3,2,0:T(8,128)(2,1)} %get-tuple-element.180, s32[]{:T(128)} %get-tuple-element.179, bf16[4,256,4096]{1,2,0:T(8,128)(2,1)} %get-tuple-element.166, bf16[4,4096,128]{1,2,0:T(8,128)(2,1)} %get-tuple-element.192, f32[256,4]{0,1:T(4,128)S(1)} %bitcast.120), kind=kOutput, calls=%fused_computation.18.clone.1 | convolution fusion | flops 1074003968 | bytes 9704448 | tf_op jit(solution)/shard_map/while/body/eval_jaxpr/grk,kd->rgd/dot_general | solution.py:48
  366.5 3.4 or_and_fusion.2
  370.0 11.6 %fusion.85 = (f32[4,256]{1,0:T(4,128)S(1)}, bf16[4,256,4096]{1,2,0:T(8,128)(2,1)}) fusion(pred[256,4096]{0,1:T(8,128)(4,1)S(1)} %or_and_fusion.2, bf16[4,4096,128]{2,1,0:T(8,128)(2,1)} %get-tuple-element.193, s32[]{:T(128)} %get-tuple-element.179, bf16[4,256,4,128]{1,3,2,0:T(8,128)(2,1)} %get-tuple-element.194), kind=kOutput, calls=%fused_computation.55.clone.1 | convolution fusion | flops 1098911744 | bytes 11801600 | tf_op jit(solution)/shard_map/while/body/eval_jaxpr/sub | solution.py:46
  381.5 5.7 %fusion.86 = bf16[4,256,4,128]{1,3,2,0:T(8,128)(2,1)} fusion(bf16[4,256,4,128]{1,3,2,0:T(8,128)(2,1)} %get-tuple-element.180, s32[]{:T(128)} %get-tuple-element.179, bf16[4,256,4096]{1,2,0:T(8,128)(2,1)} %get-tuple-element.166, bf16[4,4096,128]{1,2,0:T(8,128)(2,1)} %get-tuple-element.192, f32[256,4]{0,1:T(4,128)S(1)} %bitcast.120), kind=kOutput, calls=%fused_computation.18.clone.1 | convolution fusion | flops 1074003968 | bytes 9704448 | tf_op jit(solution)/shard_map/while/body/eval_jaxpr/grk,kd->rgd/dot_general | solution.py:48
  387.2 3.4 or_and_fusion.2
  390.7 11.6 %fusion.85 = (f32[4,256]{1,0:T(4,128)S(1)}, bf16[4,256,4096]{1,2,0:T(8,128)(2,1)}) fusion(pred[256,4096]{0,1:T(8,128)(4,1)S(1)} %or_and_fusion.2, bf16[4,4096,128]{2,1,0:T(8,128)(2,1)} %get-tuple-element.193, s32[]{:T(128)} %get-tuple-element.179, bf16[4,256,4,128]{1,3,2,0:T(8,128)(2,1)} %get-tuple-element.194), kind=kOutput, calls=%fused_computation.55.clone.1 | convolution fusion | flops 1098911744 | bytes 11801600 | tf_op jit(solution)/shard_map/while/body/eval_jaxpr/sub | solution.py:46
  402.2 5.7 %fusion.86 = bf16[4,256,4,128]{1,3,2,0:T(8,128)(2,1)} fusion(bf16[4,256,4,128]{1,3,2,0:T(8,128)(2,1)} %get-tuple-element.180, s32[]{:T(128)} %get-tuple-element.179, bf16[4,256,4096]{1,2,0:T(8,128)(2,1)} %get-tuple-element.166, bf16[4,4096,128]{1,2,0:T(8,128)(2,1)} %get-tuple-element.192, f32[256,4]{0,1:T(4,128)S(1)} %bitcast.120), kind=kOutput, calls=%fused_computation.18.clone.1 | convolution fusion | flops 1074003968 | bytes 9704448 | tf_op jit(solution)/shard_map/while/body/eval_jaxpr/grk,kd->rgd/dot_general | solution.py:48
  (29 shorter events, 16.5 us)
Async XLA Ops:
  6.5 137.6 %copy-start = (bf16[256,3584]{1,0:T(8,128)(2,1)S(1)}, bf16[256,3584]{1,0:T(8,128)(2,1)}, u32[]{:S(2)}) copy-start(bf16[256,3584]{1,0:T(8,128)(2,1)} %param.7) | copy-start | bytes 5505028
  6.5 137.6 %all-gather.6.cloned.1.call-start = ((), (), s32[]{:S(2)}) async-start(), calls=%async_computation.1 | async-start | bytes 9175040 | tf_op jit(solution)/shard_map/all_gather | solution.py:67
  10.3 191.8 %copy-start.1 = (s32[8192]{0:T(1024)S(1)}, s32[8192]{0:T(1024)}, u32[]{:S(2)}) copy-start(s32[8192]{0:T(1024)} %param.11) | copy-start | bytes 98308
  10.3 184.4 %all-gather.4.cloned.1.call-start = ((), (), s32[]{:S(2)}) async-start(), calls=%async_computation | async-start | bytes 2621440 | tf_op jit(solution)/shard_map/all_gather | solution.py:70
  194.7 48.6 %collective-permute-start = (bf16[1024,1024]{0,1:T(8,128)(2,1)}, bf16[1024,1024]{0,1:T(8,128)(2,1)}, u32[]{:S(2)}, u32[]{:S(2)}) collective-permute-start(bf16[1024,1024]{0,1:T(8,128)(2,1)} %all-gather.4.cloned.1.call-done), channel_id=1, source_target_pairs={{0,4},{4,8},{8,12},{12,16},{16,20},{20,24},{24,28},{1,5},{5,9},{9,... | collective-permute-start | bytes 6291464 | tf_op jit(solution)/shard_map/ppermute | solution.py:17
  196.6 51.7 %collective-permute-start.1 = (bf16[1024,1024]{0,1:T(8,128)(2,1)}, bf16[1024,1024]{0,1:T(8,128)(2,1)}, u32[]{:S(2)}, u32[]{:S(2)}) collective-permute-start(bf16[1024,1024]{0,1:T(8,128)(2,1)} %all-gather.4.cloned.1.call-done), channel_id=1, source_target_pairs={{0,8},{4,12},{8,16},{12,20},{16,24},{20,28},{1,9},{5,13},{9,17},{1... | collective-permute-start | bytes 6291464 | tf_op jit(solution)/shard_map/ppermute | solution.py:17
  200.0 113.1 %collective-permute-start.2 = (bf16[1024,1024]{0,1:T(8,128)(2,1)}, bf16[1024,1024]{0,1:T(8,128)(2,1)}, u32[]{:S(2)}, u32[]{:S(2)}) collective-permute-start(bf16[1024,1024]{0,1:T(8,128)(2,1)} %all-gather.4.cloned.1.call-done), channel_id=1, source_target_pairs={{0,12},{4,16},{8,20},{12,24},{16,28},{1,13},{5,17},{9,21},{13,25},... | collective-permute-start | bytes 6291464 | tf_op jit(solution)/shard_map/ppermute | solution.py:17
  202.1 24.8 %copy-start.2 = (bf16[256,2048]{1,0:T(8,128)(2,1)S(1)}, bf16[256,2048]{1,0:T(8,128)(2,1)}, u32[]{:S(2)}) copy-start(bf16[256,2048]{1,0:T(8,128)(2,1)} %param.8) | copy-start | bytes 3145732
Sparse Core Ops, SparseCore 0:
  10.4 133.6 all-gather.5
  150.3 44.4 all-gather.3
where the time goes:
time: 418 us; the launch traced here: 417 us
  waiting for transfers between devices  258 us (62%)
  matrix products  75 us (18%)
  local copies, waits for them, and re-layouts  48.6 us (12%)
  between operations  14.4 us (3%)
  other arithmetic  13.9 us (3%)
  starting transfers between devices  7.25 us (2%)
    all_gather x1, waiting for transfers between devices, local(): lax.all_gather(own_weight, 'fsdp', axis=0, tiled=True)  134 us
    ppermute x3, waiting for transfers between devices, from_behind(): return lax.ppermute(block, axis, route)  79.5 us
    sub x4, matrix products, one_head(): weights = jnp.where(allowed[None], jnp.exp(scores - highest), 0.0)  46.3 us
    all_gather x1, waiting for transfers between devices, local(): block_kv = lax.all_gather(own_kv, 'fsdp', axis=0, tiled=True)  44.6 us
    gather x1, local copies, waits for them, and re-layouts, build_mask(): key_doc = jnp.where(key_pos >= 0, doc_ids[jnp.maximum(key_pos, 0)], -1)  23 us
    dot_general x4, matrix products, one_head(): jnp.einsum('grk,kd->rgd', weights.astype(jnp.bfloat16), head_v, preferred...  22.7 us
    and x4, other arithmetic, build_mask(): return jnp.logical_and(same_doc, jnp.logical_or(earlier, own_image))  13.8 us
  transfers between devices with their start and end apart: 5, of which 5 were waited for; matrix products, arithmetic and copies ran while one was open for 8% of the time, Pallas kernels for 0%

commit v1 on v0

v1 whole, which is shorter than its diff:
```python
import functools
import math

import jax
import jax.numpy as jnp
from jax import lax
from jax.experimental import pallas as pl
from jax.experimental.pallas import tpu as pltpu
from jax.sharding import PartitionSpec as P

KVH = 4
HD = 128
QH = 16
SPAN = 3
NEG = -1e30


def from_behind(block, axis, distance):
    devices = range(lax.axis_size(axis))
    route = [(i - distance, i) for i in devices if i - distance in devices]
    return lax.ppermute(block, axis, route)


def attend_kernel(key_block, marks, lo_ref, hi_ref, q_ref, k_ref, v_ref, out_ref, qt, top, total, acc):
    rows = q_ref.shape[0]
    per_group = QH // KVH
    factor = math.log2(math.e) / math.sqrt(HD)
    for g in range(per_group):
        qt[:, g * rows : (g + 1) * rows] = q_ref[:, g * HD : (g + 1) * HD].T
    top[...] = jnp.full_like(top, NEG)
    total[...] = jnp.zeros_like(total)
    acc[...] = jnp.zeros_like(acc)

    def step(masked, b, _):
        at = pl.multiple_of(b * key_block, key_block)
        keys = k_ref[pl.ds(at, key_block), :]
        values = v_ref[pl.ds(at, key_block), :]
        if masked:
            place = at + lax.broadcasted_iota(jnp.int32, (key_block, rows), 0)
            allowed = jnp.logical_and(place >= lo_ref[...], place <= hi_ref[...])
        for g in range(per_group):
            lanes = slice(g * rows, (g + 1) * rows)
            scores = jnp.dot(keys, qt[:, lanes], preferred_element_type=jnp.float32)
            if masked:
                scores = jnp.where(allowed, scores, NEG)
            before = top[:, lanes]
            peak = jnp.maximum(before, jnp.max(scores, axis=0, keepdims=True))
            weights = jnp.exp2((scores - peak) * factor)
            shrink = jnp.exp2((before - peak) * factor)
            top[:, lanes] = peak
            total[:, lanes] = total[:, lanes] * shrink + jnp.sum(weights, axis=0, keepdims=True)
            acc[:, lanes] = acc[:, lanes] * shrink + lax.dot_general(
                values,
                weights.astype(jnp.bfloat16),
                (((0,), (0,)), ((), ())),
                preferred_element_type=jnp.float32,
            )
        return 0

    first, full_first, full_end, end = marks[0], marks[1], marks[2], marks[3]
    lax.fori_loop(first, full_first, functools.partial(step, True), 0)
    lax.fori_loop(full_first, full_end, functools.partial(step, False), 0)
    lax.fori_loop(full_end, end, functools.partial(step, True), 0)
    for g in range(per_group):
        lanes = slice(g * rows, (g + 1) * rows)
        mixed = (acc[:, lanes] / total[:, lanes]).T
        out_ref[:, g * HD : (g + 1) * HD] = mixed.astype(out_ref.dtype)


def attend(queries, window, lo, hi):
    rows = queries.shape[0]
    n_keys = window.shape[0]
    key_block = math.gcd(n_keys, 512)
    per_group = QH // KVH
    lo_min, lo_max, hi_min, hi_max = jnp.min(lo), jnp.max(lo), jnp.min(hi), jnp.max(hi)
    first = lo_min // key_block
    end = hi_max // key_block + 1
    full_first = jnp.minimum((lo_max + key_block - 1) // key_block, end)
    full_end = jnp.maximum((hi_min + 1) // key_block, full_first)
    marks = jnp.stack([first, full_first, full_end, end]).astype(jnp.int32)
    wide = per_group * HD
    return pl.pallas_call(
        functools.partial(attend_kernel, key_block),
        grid=(KVH,),
        in_specs=[
            pl.BlockSpec(memory_space=pltpu.SMEM),
            pl.BlockSpec((1, rows), lambda h: (0, 0)),
            pl.BlockSpec((1, rows), lambda h: (0, 0)),
            pl.BlockSpec((rows, wide), lambda h: (0, h)),
            pl.BlockSpec((n_keys, HD), lambda h: (0, h)),
            pl.BlockSpec((n_keys, HD), lambda h: (0, KVH + h)),
        ],
        out_specs=pl.BlockSpec((rows, wide), lambda h: (0, h)),
        out_shape=jax.ShapeDtypeStruct(queries.shape, queries.dtype),
        scratch_shapes=[
            pltpu.VMEM((HD, per_group * rows), jnp.bfloat16),
            pltpu.VMEM((1, per_group * rows), jnp.float32),
            pltpu.VMEM((1, per_group * rows), jnp.float32),
            pltpu.VMEM((HD, per_group * rows), jnp.float32),
        ],
        name="attend",
    )(marks, lo[None, :], hi[None, :], queries, window, window)


def key_range(doc_ids, rows, block_rows, seq_place, fsdp_place, modality):
    start = seq_place * block_rows + fsdp_place * rows
    here = lax.dynamic_slice_in_dim(doc_ids, start, rows, 0)
    query_pos = start + jnp.arange(rows, dtype=jnp.int32)
    below = jnp.sum((doc_ids[None, :] < here[:, None]).astype(jnp.int32), axis=1)
    upto = jnp.sum((doc_ids[None, :] <= here[:, None]).astype(jnp.int32), axis=1)
    last = jnp.minimum(upto - 1, (seq_place + 1) * block_rows - 1)
    base = (seq_place - SPAN) * block_rows
    lo = below - base
    hi = jnp.where(modality == 1, last, query_pos) - base
    return lo, hi


def local(hidden, queries, kv_weights, image_groups, doc_ids):
    rows = hidden.shape[0]
    block_rows = rows * lax.axis_size("fsdp")
    seq_place = lax.axis_index("seq")
    fsdp_place = lax.axis_index("fsdp")
    modality = image_groups[0]
    lo, hi = key_range(doc_ids, rows, block_rows, seq_place, fsdp_place, modality)
    own_weight = lax.dynamic_index_in_dim(kv_weights, modality, 0, keepdims=False)
    own_kv = jnp.dot(
        hidden,
        lax.all_gather(own_weight, "fsdp", axis=0, tiled=True),
        preferred_element_type=jnp.float32,
    ).astype(jnp.bfloat16)
    block_kv = lax.all_gather(own_kv, "fsdp", axis=0, tiled=True)
    pieces = [from_behind(block_kv, "seq", offset) for offset in range(SPAN, 0, -1)]
    window = jnp.concatenate(pieces + [block_kv], 0)
    return attend(queries, window, lo, hi)


def solution(mesh):
    in_specs = (
        P(("seq", "fsdp"), None),
        P(("seq", "fsdp"), None),
        P(None, "fsdp", None),
        P("seq"),
        P(),
    )
    out_specs = P(("seq", "fsdp"), None)
    return jax.shard_map(local, mesh=mesh, in_specs=in_specs, out_specs=out_specs, check_vma=False)
```

time: 418 us -> 382 us (0.914)
  matrix products: 75 us -> 5.94 us
  Pallas kernels: 0 us -> 52.8 us
  local copies, waits for them, and re-layouts: 48.6 us -> 3.06 us
  waiting for transfers between devices: 258 us -> 277 us
  between operations: 14.4 us -> 21 us
    pallas_call x0 -> x1, Pallas kernels: none -> 52.8 us  [attend(): pl.pallas_call(functools.partial(attend_kernel, key_block), grid=(KVH,),...]
    sub x4 -> x0, matrix products: 46.3 us -> none  [one_head(): weights = jnp.where(allowed[None], jnp.exp(scores - highest), 0.0)]
    gather x2 -> x0, local copies, waits for them, and re-layouts: 24.8 us -> none  [the longest x1 23 us: build_mask(): key_doc = jnp.where(key_pos >= 0, doc_ids[jnp.maximum(key_pos, 0)], -1)]
    dot_general x4 -> x0, matrix products: 22.7 us -> none  [one_head(): jnp.einsum('grk,kd->rgd', weights.astype(jnp.bfloat16), head_v, preferred...]
    ppermute x3, waiting for transfers between devices: 79.5 us -> 99.1 us  [from_behind(): return lax.ppermute(block, axis, route)]
    and x5 -> x0, other arithmetic: 13.8 us -> none  [the longest x4 13.8 us: build_mask(): return jnp.logical_and(same_doc, jnp.logical_or(earlier, own_image))]
    reshape x2 -> x0, local copies, waits for them, and re-layouts: 8.63 us -> none  [the longest x1 6.37 us: attend(): keys_values[:, :KVH * HD].reshape(n_keys, KVH, HD).transpose(1, 0, 2)]
    concatenate x0 -> x1, other arithmetic: none -> 7.12 us  [local(): window = jnp.concatenate(pieces + [block_kv], 0)]
  transfers between devices with their start and end apart: 5 -> 5, of which waited for: 5 -> 5; matrix products, arithmetic and copies ran while one was open for 8% -> 1% of each run, Pallas kernels for 0% -> 0%
where the time goes in v1:
time: 382 us; the launch traced here: 379 us
  waiting for transfers between devices  277 us (73%)
  Pallas kernels  52.8 us (14%)
  between operations  21 us (5%)
  other arithmetic  12.3 us (3%)
  starting transfers between devices  7.25 us (2%)
  matrix products  5.94 us (2%)
    all_gather x1, waiting for transfers between devices, local(): lax.all_gather(own_weight, 'fsdp', axis=0, tiled=True)  134 us
    ppermute x3, waiting for transfers between devices, from_behind(): return lax.ppermute(block, axis, route)  99.1 us
    pallas_call x1, Pallas kernels, attend(): pl.pallas_call(functools.partial(attend_kernel, key_block), grid=(KVH,),...  52.8 us
    all_gather x1, waiting for transfers between devices, local(): block_kv = lax.all_gather(own_kv, 'fsdp', axis=0, tiled=True)  44 us
  transfers between devices with their start and end apart: 5, of which 5 were waited for; matrix products, arithmetic and copies ran while one was open for 1% of the time, Pallas kernels for 0%

profile of v1, /device:TPU:4, one launch (start us, length us, event | category | flops | bytes accessed | tf_op | source)
XLA Modules:
  0.0 379.3 jit_solution(6717086547341000459)
XLA Ops:
  7.3 3.0 constant_dynamic-slice_fusion
  10.3 0.0 all-gather.6.cloned.1.call-update
  10.3 0.0 copy-start.1
  10.3 0.0 all-gather.4.cloned.1.call-start
  10.4 133.8 %all-gather.6.cloned.1.call-done = bf16[1,3584,1024]{2,1,0:T(8,128)(2,1)} async-done(((bf16[1,896,1024]{2,1,0:T(8,128)(2,1)}), bf16[1,3584,1024]{2,1,0:T(8,128)(2,1)}) %all-gather.6.cloned.1.call-update) | async-done | bytes 7340048 | tf_op jit(solution)/shard_map/all_gather | solution.py:128
  144.2 0.0 copy-done
  144.2 5.9 %fusion.5 = bf16[256,1024]{1,0:T(8,128)(2,1)} fusion(bf16[256,3584]{1,0:T(8,128)(2,1)S(1)} %copy-done, bf16[1,3584,1024]{2,1,0:T(8,128)(2,1)} %all-gather.6.cloned.1.call-done), kind=kOutput, calls=%fused_computation.6 | convolution fusion | flops 1879310336 | bytes 9699328 | tf_op jit(solution)/shard_map/dot_general | solution.py:126
  150.1 0.0 all-gather.4.cloned.1.call-update
  150.1 44.0 %all-gather.4.cloned.1.call-done = bf16[1024,1024]{1,0:T(8,128)(2,1)} async-done(((bf16[256,1024]{1,0:T(8,128)(2,1)}), bf16[1024,1024]{1,0:T(8,128)(2,1)}) %all-gather.4.cloned.1.call-update) | async-done | bytes 2097168 | tf_op jit(solution)/shard_map/all_gather | solution.py:131
  194.1 1.9 collective-permute-start.2
  196.0 3.4 collective-permute-start.1
  199.4 1.9 collective-permute-start
  201.4 0.0 copy-done.1
  201.4 0.1 dynamic_slice.7
  201.4 2.0 convert_reduce_fusion.1
  203.4 1.3 fusion.11
  208.0 0.7 fusion.9
  212.3 0.6 pad_add_fusion.marks
  212.9 0.6 fusion.8.hi_ref
  213.5 29.3 %collective-permute-done.2 = bf16[1024,1024]{1,0:T(8,128)(2,1)} collective-permute-done((bf16[1024,1024]{1,0:T(8,128)(2,1)}, bf16[1024,1024]{1,0:T(8,128)(2,1)}, u32[]{:S(2)}, u32[]{:S(2)}) %collective-permute-start.2) | collective-permute-done | bytes 2097184 | tf_op jit(solution)/shard_map/ppermute | solution.py:21
  242.7 5.0 %collective-permute-done.1 = bf16[1024,1024]{1,0:T(8,128)(2,1)} collective-permute-done((bf16[1024,1024]{1,0:T(8,128)(2,1)}, bf16[1024,1024]{1,0:T(8,128)(2,1)}, u32[]{:S(2)}, u32[]{:S(2)}) %collective-permute-start.1) | collective-permute-done | bytes 2097184 | tf_op jit(solution)/shard_map/ppermute | solution.py:21
  247.7 64.8 %collective-permute-done = bf16[1024,1024]{1,0:T(8,128)(2,1)} collective-permute-done((bf16[1024,1024]{1,0:T(8,128)(2,1)}, bf16[1024,1024]{1,0:T(8,128)(2,1)}, u32[]{:S(2)}, u32[]{:S(2)}) %collective-permute-start) | collective-permute-done | bytes 2097184 | tf_op jit(solution)/shard_map/ppermute | solution.py:21
  312.6 7.1 %pad_maximum_fusion.k_ref.v_ref = bf16[4096,1024]{1,0:T(8,128)(2,1)} fusion(bf16[1024,1024]{1,0:T(8,128)(2,1)} %all-gather.4.cloned.1.call-done, bf16[1024,1024]{1,0:T(8,128)(2,1)} %collective-permute-done.2, bf16[1024,1024]{1,0:T(8,128)(2,1)} %collective-permute-done.1, bf16[1024,1024]{1,0:T(8,128)(2,1)} %collective-permute-done), kind=kLoop, calls=%fused_computation | loop fusion | flops 33554432 | bytes 16777216 | tf_op jit(solution)/shard_map/concatenate | solution.py:133
  319.7 52.8 %attend.1 = bf16[256,2048]{1,0:T(8,128)(2,1)} custom-call(s32[4]{0:T(128)} %pad_add_fusion.marks, s32[1,256]{1,0:T(1,128)} %bitcast.21, s32[1,256]{1,0:T(1,128)} %fusion.8.hi_ref, bf16[256,2048]{1,0:T(8,128)(2,1)} %q_ref.1, bf16[4096,1024]{1,0:T(8,128)(2,1)} %pad_maximum_fusion.k_ref.v_ref, bf16[4096,1024]{1,0:T(8,128)(2,1)} %pad_maximum_fusion.k_ref.v_ref), custom_call_target="tpu_custom_call" | custom-call | tf_op jit(solution)/shard_map/attend/pallas_call | solution.py:82
  (2 shorter events, 0.0 us)
Async XLA Ops:
  6.5 137.6 %copy-start = (bf16[256,3584]{1,0:T(8,128)(2,1)S(1)}, bf16[256,3584]{1,0:T(8,128)(2,1)}, u32[]{:S(2)}) copy-start(bf16[256,3584]{1,0:T(8,128)(2,1)} %param.5) | copy-start | bytes 5505028
  6.5 137.6 %all-gather.6.cloned.1.call-start = ((), (), s32[]{:S(2)}) async-start(), calls=%async_computation.1 | async-start | bytes 9175040 | tf_op jit(solution)/shard_map/all_gather | solution.py:128
  10.3 191.0 %copy-start.1 = (s32[8192]{0:T(1024)S(1)}, s32[8192]{0:T(1024)}, u32[]{:S(2)}) copy-start(s32[8192]{0:T(1024)} %param.9) | copy-start | bytes 98308
  10.3 183.8 %all-gather.4.cloned.1.call-start = ((), (), s32[]{:S(2)}) async-start(), calls=%async_computation | async-start | bytes 2621440 | tf_op jit(solution)/shard_map/all_gather | solution.py:131
  194.1 48.6 %collective-permute-start.2 = (bf16[1024,1024]{1,0:T(8,128)(2,1)}, bf16[1024,1024]{1,0:T(8,128)(2,1)}, u32[]{:S(2)}, u32[]{:S(2)}) collective-permute-start(bf16[1024,1024]{1,0:T(8,128)(2,1)} %all-gather.4.cloned.1.call-done), channel_id=1, source_target_pairs={{0,4},{4,8},{8,12},{12,16},{16,20},{20,24},{24,28},{1,5},{5,9},{9,... | collective-permute-start | bytes 6291464 | tf_op jit(solution)/shard_map/ppermute | solution.py:21
  196.0 51.7 %collective-permute-start.1 = (bf16[1024,1024]{1,0:T(8,128)(2,1)}, bf16[1024,1024]{1,0:T(8,128)(2,1)}, u32[]{:S(2)}, u32[]{:S(2)}) collective-permute-start(bf16[1024,1024]{1,0:T(8,128)(2,1)} %all-gather.4.cloned.1.call-done), channel_id=1, source_target_pairs={{0,8},{4,12},{8,16},{12,20},{16,24},{20,28},{1,9},{5,13},{9,17},{1... | collective-permute-start | bytes 6291464 | tf_op jit(solution)/shard_map/ppermute | solution.py:21
  199.4 113.1 %collective-permute-start = (bf16[1024,1024]{1,0:T(8,128)(2,1)}, bf16[1024,1024]{1,0:T(8,128)(2,1)}, u32[]{:S(2)}, u32[]{:S(2)}) collective-permute-start(bf16[1024,1024]{1,0:T(8,128)(2,1)} %all-gather.4.cloned.1.call-done), channel_id=1, source_target_pairs={{0,12},{4,16},{8,20},{12,24},{16,28},{1,13},{5,17},{9,21},{13,25},... | collective-permute-start | bytes 6291464 | tf_op jit(solution)/shard_map/ppermute | solution.py:21
Sparse Core Ops, SparseCore 0:
  10.4 133.6 all-gather.5
  150.2 43.8 all-gather.3

commit v2 on v1

--- a/solution.py
+++ b/solution.py
@@ -115,6 +115,160 @@
     return lo, hi
 
 
+def flip(place, bits):
+    out = place
+    bit = 1
+    while bit <= bits:
+        if bits & bit:
+            out = out + bit * (1 - 2 * (lax.div(place, bit) % 2))
+        bit *= 2
+    return out
+
+
+def project_kernel(slices, fsdp, mod_ref, hidden_ref, w_ref, out_ref, held, acc, send, recv):
+    seq_place = lax.axis_index("seq")
+    fsdp_place = lax.axis_index("fsdp")
+    depth = w_ref.shape[1]
+    width = w_ref.shape[2] // slices
+    place = seq_place % slices
+    base = seq_place - place
+    odd = place % 2
+    near = 2 + 2 * odd
+    far = 4 - 2 * odd
+
+    def step_over(value, bit):
+        return value + bit * (1 - 2 * (lax.div(value, bit) % 2))
+
+    near_place = step_over(place, near)
+    far_place = step_over(place, far)
+    both_place = step_over(near_place, far)
+    twin_place = flip(place, 1)
+    own_places = (place, near_place, far_place, both_place)
+    twin_near = flip(far_place, 1)
+    twin_far = flip(near_place, 1)
+    twin_places = (twin_place, twin_near, twin_far, flip(both_place, 1))
+
+    barrier = pltpu.get_barrier_semaphore()
+    greeted = [(seq_place, flip(fsdp_place, d)) for d in range(1, fsdp)]
+    greeted += [(base + other, fsdp_place) for other in (near_place, far_place, twin_place)]
+    for device in greeted:
+        pl.semaphore_signal(barrier, inc=1, device_id=device, device_id_type=pl.DeviceIdType.MESH)
+    pl.semaphore_wait(barrier, len(greeted))
+
+    def first(d):
+        return pltpu.make_async_remote_copy(
+            src_ref=w_ref.at[:, :, pl.ds(pl.multiple_of(place * width, width), width)],
+            dst_ref=held.at[d - 1, 0],
+            send_sem=send.at[d - 1, 0],
+            recv_sem=recv.at[d - 1, 0],
+            device_id=(seq_place, flip(fsdp_place, d)),
+            device_id_type=pl.DeviceIdType.MESH,
+        )
+
+    def onward(d, source, target, other, number):
+        return pltpu.make_async_remote_copy(
+            src_ref=held.at[d - 1, source],
+            dst_ref=held.at[d - 1, target],
+            send_sem=send.at[d - 1, number],
+            recv_sem=recv.at[d - 1, target],
+            device_id=(base + other, fsdp_place),
+            device_id_type=pl.DeviceIdType.MESH,
+        )
+
+    def copies(d):
+        return {
+            "first": first(d),
+            "near": onward(d, 0, 1, near_place, 1),
+            "far": onward(d, 0, 2, far_place, 2),
+            "both": onward(d, 1, 3, far_place, 3),
+            "twin0": onward(d, 0, 4, twin_place, 4),
+            "twin1": onward(d, 1, 5, twin_place, 5),
+            "twin2": onward(d, 2, 6, twin_place, 6),
+            "twin3": onward(d, 3, 7, twin_place, 7),
+        }
+
+    plan = {d: copies(d) for d in range(1, fsdp)}
+    for d in range(1, fsdp):
+        plan[d]["first"].start()
+
+    image = mod_ref[0] == 1
+
+    def add(d, slot, at):
+        weight = jnp.where(image, held[d - 1, slot, 1], held[d - 1, slot, 0])
+        rows = hidden_ref[:, pl.ds(pl.multiple_of(flip(fsdp_place, d) * depth, 128), depth)]
+        acc[at] += jnp.dot(rows, weight, preferred_element_type=jnp.float32)
+
+    own_rows = hidden_ref[:, pl.ds(pl.multiple_of(fsdp_place * depth, 128), depth)]
+    for at in range(slices):
+        columns = slice(at * width, (at + 1) * width)
+        weight = jnp.where(image, w_ref[1, :, columns], w_ref[0, :, columns])
+        acc[at] = jnp.dot(own_rows, weight, preferred_element_type=jnp.float32)
+
+    def got_first(d):
+        plan[d]["first"].wait_recv()
+        plan[d]["near"].start()
+        plan[d]["far"].start()
+        plan[d]["twin0"].start()
+
+    def got_near(d):
+        plan[d]["near"].wait_recv()
+        plan[d]["both"].start()
+        plan[d]["twin1"].start()
+
+    def got_far(d):
+        plan[d]["far"].wait_recv()
+        plan[d]["twin2"].start()
+        plan[d]["both"].wait_recv()
+        plan[d]["twin3"].start()
+
+    def use(d):
+        for slot in range(4):
+            add(d, slot, own_places[slot])
+        for slot in range(4):
+            plan[d]["twin%d" % slot].wait_recv()
+            add(d, 4 + slot, twin_places[slot])
+
+    got_first(1)
+    for d in range(1, fsdp):
+        got_near(d)
+        if d + 1 < fsdp:
+            got_first(d + 1)
+        got_far(d)
+        if d > 1:
+            use(d - 1)
+    use(fsdp - 1)
+    for at in range(slices):
+        out_ref[:, at * width : (at + 1) * width] = acc[at].astype(out_ref.dtype)
+    for d in range(1, fsdp):
+        for copy in plan[d].values():
+            copy.wait_send()
+
+
+def project(hidden, kv_weights, image_groups):
+    fsdp = lax.axis_size("fsdp")
+    rows = hidden.shape[0]
+    _, depth, kv_width = kv_weights.shape
+    slices = 8
+    width = kv_width // slices
+    vmem = pl.BlockSpec(memory_space=pltpu.VMEM)
+    return pl.pallas_call(
+        functools.partial(project_kernel, slices, fsdp),
+        in_specs=[pl.BlockSpec(memory_space=pltpu.SMEM), vmem, vmem],
+        out_specs=vmem,
+        out_shape=jax.ShapeDtypeStruct((rows, kv_width), jnp.bfloat16),
+        scratch_shapes=[
+            pltpu.VMEM((fsdp - 1, slices, 2, depth, width), jnp.bfloat16),
+            pltpu.VMEM((slices, rows, width), jnp.float32),
+            pltpu.SemaphoreType.DMA((fsdp - 1, slices)),
+            pltpu.SemaphoreType.DMA((fsdp - 1, slices)),
+        ],
+        compiler_params=pltpu.CompilerParams(
+            collective_id=0, has_side_effects=True, vmem_limit_bytes=48 * 1024 * 1024
+        ),
+        name="project",
+    )(image_groups, hidden, kv_weights)
+
+
 def local(hidden, queries, kv_weights, image_groups, doc_ids):
     rows = hidden.shape[0]
     block_rows = rows * lax.axis_size("fsdp")
@@ -122,12 +276,7 @@
     fsdp_place = lax.axis_index("fsdp")
     modality = image_groups[0]
     lo, hi = key_range(doc_ids, rows, block_rows, seq_place, fsdp_place, modality)
-    own_weight = lax.dynamic_index_in_dim(kv_weights, modality, 0, keepdims=False)
-    own_kv = jnp.dot(
-        hidden,
-        lax.all_gather(own_weight, "fsdp", axis=0, tiled=True),
-        preferred_element_type=jnp.float32,
-    ).astype(jnp.bfloat16)
+    own_kv = project(hidden, kv_weights, image_groups)
     block_kv = lax.all_gather(own_kv, "fsdp", axis=0, tiled=True)
     pieces = [from_behind(block_kv, "seq", offset) for offset in range(SPAN, 0, -1)]
     window = jnp.concatenate(pieces + [block_kv], 0)

time: 382 us -> 302 us (0.79)
  waiting for transfers between devices: 277 us -> 143 us
  Pallas kernels: 52.8 us -> 115 us
  matrix products: 5.94 us -> 0 us
    all_gather x1 -> x0, waiting for transfers between devices: 134 us -> none  [local(): lax.all_gather(own_weight, 'fsdp', axis=0, tiled=True)]
    pallas_call x0 -> x1, Pallas kernels: none -> 76.6 us  [project(): pl.pallas_call(functools.partial(project_kernel, slices, fsdp), in_specs=...]
    pallas_call x1, Pallas kernels: 52.8 us -> 38.9 us  [attend(): pl.pallas_call(functools.partial(attend_kernel, key_block), grid=(KVH,),...]
    dot_general x1 -> x0, matrix products: 5.94 us -> none  [local(): jnp.dot(hidden, lax.all_gather(own_weight, 'fsdp', axis=0, tiled=True), p...]
  transfers between devices with their start and end apart: 5 -> 4, of which waited for: 5 -> 4; matrix products, arithmetic and copies ran while one was open for 1% -> 2% of each run, Pallas kernels for 0% -> 0%
where the time goes in v2:
time: 302 us
  waiting for transfers between devices  143 us (47%)
  Pallas kernels  115 us (38%)
  between operations  20.3 us (7%)
  other arithmetic  11.7 us (4%)
  starting transfers between devices  7.39 us (2%)
  local copies, waits for them, and re-layouts  4.29 us (1%)
    ppermute x3, waiting for transfers between devices, from_behind(): return lax.ppermute(block, axis, route)  99 us
    pallas_call x1, Pallas kernels, project(): pl.pallas_call(functools.partial(project_kernel, slices, fsdp), in_specs=...  76.6 us
    all_gather x1, waiting for transfers between devices, local(): block_kv = lax.all_gather(own_kv, 'fsdp', axis=0, tiled=True)  43.7 us
    pallas_call x1, Pallas kernels, attend(): pl.pallas_call(functools.partial(attend_kernel, key_block), grid=(KVH,),...  38.9 us
    ppermute x3, starting transfers between devices, from_behind(): return lax.ppermute(block, axis, route)  7.39 us
    concatenate x1, other arithmetic, local(): window = jnp.concatenate(pieces + [block_kv], 0)  6.59 us
  transfers between devices with their start and end apart: 4, of which 4 were waited for; matrix products, arithmetic and copies ran while one was open for 2% of the time, Pallas kernels for 0%

profile of v2, /device:TPU:4, one launch (start us, length us, event | category | flops | bytes accessed | tf_op | source)
XLA Modules:
  0.0 301.8 jit_solution(3376354165543738538)
XLA Ops:
  6.5 0.0 all-gather.2.cloned.1.call-start
  7.2 0.0 copy-start
  7.2 2.0 copy-done
  9.2 0.0 copy-start.1
  9.2 1.5 copy-done.1
  10.7 76.6 %project.1 = bf16[256,1024]{1,0:T(8,128)(2,1)} custom-call(s32[1]{0:T(128)S(6)} %copy.6.mod_ref, bf16[256,3584]{1,0:T(8,128)(2,1)S(1)} %copy-done.1, bf16[2,896,1024]{2,1,0:T(8,128)(2,1)S(1)} %copy-done), custom_call_target="tpu_custom_call" | custom-call | tf_op jit(solution)/shard_map/project/pallas_call | solution.py:254
  87.3 0.0 all-gather.2.cloned.1.call-update
  87.4 43.7 %all-gather.2.cloned.1.call-done = bf16[1024,1024]{1,0:T(8,128)(2,1)} async-done(((bf16[256,1024]{1,0:T(8,128)(2,1)}), bf16[1024,1024]{1,0:T(8,128)(2,1)}) %all-gather.2.cloned.1.call-update) | async-done | bytes 2097168 | tf_op jit(solution)/shard_map/all_gather | solution.py:280
  131.1 1.9 collective-permute-start.2
  133.0 3.4 %collective-permute-start.1 = (bf16[1024,1024]{1,0:T(8,128)(2,1)}, bf16[1024,1024]{1,0:T(8,128)(2,1)}, u32[]{:S(2)}, u32[]{:S(2)}) collective-permute-start(bf16[1024,1024]{1,0:T(8,128)(2,1)} %all-gather.2.cloned.1.call-done), channel_id=1, source_target_pairs={{0,8},{4,12},{8,16},{12,20},{16,24},{20,28},{1,9},{5,13},{9,17},{1... | collective-permute-start | bytes 6291464 | tf_op jit(solution)/shard_map/ppermute | solution.py:21
  136.4 2.1 collective-permute-start
  138.5 0.8 dynamic_slice.3
  139.3 2.5 convert_reduce_fusion.1
  141.8 1.3 fusion.1
  149.3 0.6 pad_add_fusion.marks
  149.9 0.6 fusion.hi_ref
  150.5 29.1 %collective-permute-done.2 = bf16[1024,1024]{1,0:T(8,128)(2,1)S(1)} collective-permute-done((bf16[1024,1024]{1,0:T(8,128)(2,1)}, bf16[1024,1024]{1,0:T(8,128)(2,1)S(1)}, u32[]{:S(2)}, u32[]{:S(2)}) %collective-permute-start.2) | collective-permute-done | bytes 2097184 | tf_op jit(solution)/shard_map/ppermute | solution.py:21
  179.6 5.1 %collective-permute-done.1 = bf16[1024,1024]{1,0:T(8,128)(2,1)} collective-permute-done((bf16[1024,1024]{1,0:T(8,128)(2,1)}, bf16[1024,1024]{1,0:T(8,128)(2,1)}, u32[]{:S(2)}, u32[]{:S(2)}) %collective-permute-start.1) | collective-permute-done | bytes 2097184 | tf_op jit(solution)/shard_map/ppermute | solution.py:21
  184.7 64.8 %collective-permute-done = bf16[1024,1024]{1,0:T(8,128)(2,1)} collective-permute-done((bf16[1024,1024]{1,0:T(8,128)(2,1)}, bf16[1024,1024]{1,0:T(8,128)(2,1)}, u32[]{:S(2)}, u32[]{:S(2)}) %collective-permute-start) | collective-permute-done | bytes 2097184 | tf_op jit(solution)/shard_map/ppermute | solution.py:21
  249.5 6.6 %pad_maximum_fusion.k_ref.v_ref = bf16[4096,1024]{1,0:T(8,128)(2,1)} fusion(bf16[1024,1024]{1,0:T(8,128)(2,1)} %all-gather.2.cloned.1.call-done, bf16[1024,1024]{1,0:T(8,128)(2,1)S(1)} %collective-permute-done.2, bf16[1024,1024]{1,0:T(8,128)(2,1)} %collective-permute-done.1, bf16[1024,1024]{1,0:T(8,128)(2,1)} %collective-permute-done), kind=kLoop, calls=%fused_computation | loop fusion | flops 33554432 | bytes 16777216 | tf_op jit(solution)/shard_map/concatenate | solution.py:282
  256.1 38.9 %attend.1 = bf16[256,2048]{1,0:T(8,128)(2,1)} custom-call(s32[4]{0:T(128)} %pad_add_fusion.marks, s32[1,256]{1,0:T(1,128)} %bitcast.7, s32[1,256]{1,0:T(1,128)} %fusion.hi_ref, bf16[256,2048]{1,0:T(8,128)(2,1)} %q_ref.1, bf16[4096,1024]{1,0:T(8,128)(2,1)} %pad_maximum_fusion.k_ref.v_ref, bf16[4096,1024]{1,0:T(8,128)(2,1)} %pad_maximum_fusion.k_ref.v_ref), custom_call_target="tpu_custom_call" | custom-call | tf_op jit(solution)/shard_map/attend/pallas_call | solution.py:82
Async XLA Ops:
  6.5 124.6 %all-gather.2.cloned.1.call-start = ((), (), s32[]{:S(2)}) async-start(), calls=%async_computation | async-start | bytes 2621440 | tf_op jit(solution)/shard_map/all_gather | solution.py:280
  7.2 2.0 copy-start
  9.2 1.5 copy-start.1
  131.1 48.5 %collective-permute-start.2 = (bf16[1024,1024]{1,0:T(8,128)(2,1)}, bf16[1024,1024]{1,0:T(8,128)(2,1)S(1)}, u32[]{:S(2)}, u32[]{:S(2)}) collective-permute-start(bf16[1024,1024]{1,0:T(8,128)(2,1)} %all-gather.2.cloned.1.call-done), channel_id=1, source_target_pairs={{0,4},{4,8},{8,12},{12,16},{16,20},{20,24},{24,28},{1,5},{5,9},{9,... | collective-permute-start | bytes 6291464 | tf_op jit(solution)/shard_map/ppermute | solution.py:21
  133.0 51.7 %collective-permute-start.1 = (bf16[1024,1024]{1,0:T(8,128)(2,1)}, bf16[1024,1024]{1,0:T(8,128)(2,1)}, u32[]{:S(2)}, u32[]{:S(2)}) collective-permute-start(bf16[1024,1024]{1,0:T(8,128)(2,1)} %all-gather.2.cloned.1.call-done), channel_id=1, source_target_pairs={{0,8},{4,12},{8,16},{12,20},{16,24},{20,28},{1,9},{5,13},{9,17},{1... | collective-permute-start | bytes 6291464 | tf_op jit(solution)/shard_map/ppermute | solution.py:21
  136.4 113.1 %collective-permute-start = (bf16[1024,1024]{1,0:T(8,128)(2,1)}, bf16[1024,1024]{1,0:T(8,128)(2,1)}, u32[]{:S(2)}, u32[]{:S(2)}) collective-permute-start(bf16[1024,1024]{1,0:T(8,128)(2,1)} %all-gather.2.cloned.1.call-done), channel_id=1, source_target_pairs={{0,12},{4,16},{8,20},{12,24},{16,28},{1,13},{5,17},{9,21},{13,25},... | collective-permute-start | bytes 6291464 | tf_op jit(solution)/shard_map/ppermute | solution.py:21
Sparse Core Ops, SparseCore 0:
  87.5 43.5 all-gather.1

commit v3 on v2

--- a/solution.py
+++ b/solution.py
@@ -13,12 +13,6 @@
 QH = 16
 SPAN = 3
 NEG = -1e30
-
-
-def from_behind(block, axis, distance):
-    devices = range(lax.axis_size(axis))
-    route = [(i - distance, i) for i in devices if i - distance in devices]
-    return lax.ppermute(block, axis, route)
 
 
 def attend_kernel(key_block, marks, lo_ref, hi_ref, q_ref, k_ref, v_ref, out_ref, qt, top, total, acc):
@@ -269,6 +263,125 @@
     )(image_groups, hidden, kv_weights)
 
 
+def collect_kernel(seq, fsdp, own_ref, out_ref, send, recv, local_sem):
+    s = lax.axis_index("seq")
+    z = lax.axis_index("fsdp")
+    odd = s % 2
+    pair_odd = lax.div(s, 2) % 2
+
+    barrier = pltpu.get_barrier_semaphore()
+    greeted = [(s, flip(z, d)) for d in range(1, fsdp)]
+    greeted += [((s + o + seq) % seq, z) for o in range(-SPAN, SPAN + 1) if o]
+    for device in greeted:
+        pl.semaphore_signal(barrier, inc=1, device_id=device, device_id_type=pl.DeviceIdType.MESH)
+    pl.semaphore_wait(barrier, len(greeted))
+
+    def held(back, d):
+        return out_ref.at[SPAN - back, flip(z, d)]
+
+    def own(d):
+        return own_ref if d == 0 else held(0, d)
+
+    def copy(source, back, d, number, ahead):
+        return pltpu.make_async_remote_copy(
+            src_ref=source,
+            dst_ref=held(back, d),
+            send_sem=send.at[number, d],
+            recv_sem=recv.at[back, d],
+            device_id=((s + ahead + seq) % seq, z),
+            device_id_type=pl.DeviceIdType.MESH,
+        )
+
+    def across(d):
+        return pltpu.make_async_remote_copy(
+            src_ref=own_ref,
+            dst_ref=held(0, 0),
+            send_sem=send.at[0, d],
+            recv_sem=recv.at[0, d],
+            device_id=(s, flip(z, d)),
+            device_id_type=pl.DeviceIdType.MESH,
+        )
+
+    even = odd == 0
+    uneven = odd == 1
+    both = jnp.logical_and
+    sends = [
+        (both(even, s + 2 < seq), lambda d: copy(own(d), 2, d, 1, 2)),
+        (even, lambda d: copy(own(d), 1, d, 2, 1)),
+        (both(uneven, both(pair_odd == 0, s + 2 < seq)), lambda d: copy(own(d), 2, d, 1, 2)),
+        (both(uneven, s + 3 < seq), lambda d: copy(own(d), 3, d, 2, 3)),
+    ]
+    after_two = [
+        (both(even, s >= 2), lambda d: copy(held(2, d), 3, d, 3, 1)),
+        (both(uneven, s >= 2), lambda d: copy(held(2, d), 1, d, 3, -1)),
+    ]
+    after_three = [(both(even, both(pair_odd == 1, s >= 4)), lambda d: copy(held(3, d), 2, d, 4, -1))]
+    got_two = s >= 2
+    got_three_early = both(even, s >= 4)
+    got_three_late = both(uneven, s >= 3)
+    got_one = jnp.logical_or(uneven, s >= 2)
+
+    def each(items, d, act):
+        for holds, make in items:
+            @pl.when(holds)
+            def _(make=make):
+                act(make(d))
+
+    def start(items, d):
+        each(items, d, lambda c: c.start())
+
+    def arrived(holds, back, d):
+        @pl.when(holds)
+        def _():
+            copy(own_ref, back, d, 1, 1).wait_recv()
+
+    keep = pltpu.make_async_copy(own_ref, held(0, 0), local_sem)
+    keep.start()
+    for d in range(1, fsdp):
+        across(d).start()
+    start(sends, 0)
+
+    def relay(d):
+        arrived(got_three_early, 3, d)
+        start(after_three, d)
+        arrived(got_two, 2, d)
+        start(after_two, d)
+
+    for d in range(1, fsdp):
+        across(d).wait_recv()
+        start(sends, d)
+        relay(d - 1)
+    relay(fsdp - 1)
+    for d in range(fsdp):
+        arrived(got_three_late, 3, d)
+        arrived(got_one, 1, d)
+    keep.wait()
+    for d in range(fsdp):
+        if d:
+            across(d).wait_send()
+        each(sends + after_two + after_three, d, lambda c: c.wait_send())
+
+
+def collect(own_kv):
+    seq, fsdp = lax.axis_size("seq"), lax.axis_size("fsdp")
+    rows, width = own_kv.shape
+    anywhere = pl.BlockSpec(memory_space=pl.ANY)
+    window = pl.pallas_call(
+        functools.partial(collect_kernel, seq, fsdp),
+        in_specs=[pl.BlockSpec(memory_space=pltpu.VMEM)],
+        out_specs=anywhere,
+        out_shape=jax.ShapeDtypeStruct((SPAN + 1, fsdp, rows, width), own_kv.dtype),
+        scratch_shapes=[
+            pltpu.SemaphoreType.DMA((5, fsdp)),
+            pltpu.SemaphoreType.DMA((SPAN + 1, fsdp)),
+            pltpu.SemaphoreType.DMA,
+        ],
+        compiler_params=pltpu.CompilerParams(collective_id=1, has_side_effects=True),
+        name="collect",
+    )(own_kv)
+    return window.reshape((SPAN + 1) * fsdp * rows, width)
+
+
 def local(hidden, queries, kv_weights, image_groups, doc_ids):
     rows = hidden.shape[0]
     block_rows = rows * lax.axis_size("fsdp")
@@ -277,9 +390,7 @@
     modality = image_groups[0]
     lo, hi = key_range(doc_ids, rows, block_rows, seq_place, fsdp_place, modality)
     own_kv = project(hidden, kv_weights, image_groups)
-    block_kv = lax.all_gather(own_kv, "fsdp", axis=0, tiled=True)
-    pieces = [from_behind(block_kv, "seq", offset) for offset in range(SPAN, 0, -1)]
-    window = jnp.concatenate(pieces + [block_kv], 0)
+    window = collect(own_kv)
     return attend(queries, window, lo, hi)
 
 

time: 302 us -> 215 us (0.71)
  the two profiles are of different devices: /device:TPU:4 before, /device:TPU:13 now
where the time goes in v3:
time: 215 us; the launch traced here: 213 us
  Pallas kernels  196 us (91%)
  between operations  6.86 us (3%)
  local copies, waits for them, and re-layouts  5.09 us (2%)
  other arithmetic  4.94 us (2%)
    pallas_call x1, Pallas kernels, collect(): pl.pallas_call(functools.partial(collect_kernel, seq, fsdp), in_specs=[pl...  77.3 us
    pallas_call x1, Pallas kernels, project(): pl.pallas_call(functools.partial(project_kernel, slices, fsdp), in_specs=...  65 us
    pallas_call x1, Pallas kernels, attend(): pl.pallas_call(functools.partial(attend_kernel, key_block), grid=(KVH,),...  53.7 us
    unnamed x6, local copies, waits for them, and re-layouts  4.32 us

profile of v3, /device:TPU:13, one launch (start us, length us, event | category | flops | bytes accessed | tf_op | source)
XLA Modules:
  0.0 212.8 jit_solution(9256660243602329793)
XLA Ops:
  0.7 0.8 dynamic_slice.3
  1.4 2.5 %convert_reduce_fusion.1 = (s32[256]{0:T(256)S(1)}, s32[256]{0:T(256)S(1)}) fusion(s32[8192]{0:T(1024)} %param.9, s32[256]{0:T(256)S(1)} %dynamic_slice.3), kind=kLoop, calls=%fused_computation.1 | loop fusion | flops 12582400 | bytes 35840 | tf_op jit(solution)/shard_map/reduce_sum | solution.py:103
  4.0 1.3 fusion.1
  11.4 0.6 pad_add_fusion.marks
  12.0 0.5 fusion.hi_ref
  12.5 0.0 copy-start
  12.5 2.0 copy-done
  14.6 0.0 copy-start.2
  14.6 1.5 copy-done.2
  16.1 65.0 %project.1.own_ref = bf16[256,1024]{1,0:T(8,128)(2,1)S(1)} custom-call(s32[1]{0:T(128)S(6)} %copy.6.mod_ref, bf16[256,3584]{1,0:T(8,128)(2,1)S(1)} %copy-done.2, bf16[2,896,1024]{2,1,0:T(8,128)(2,1)S(1)} %copy-done), custom_call_target="tpu_custom_call" | custom-call | tf_op jit(solution)/shard_map/project/pallas_call | solution.py:248
  81.1 0.0 copy-start.1
  81.1 0.8 copy-done.1
  81.9 77.3 %collect.1 = bf16[4,4,256,1024]{3,2,1,0:T(8,128)(2,1)} custom-call(bf16[256,1024]{1,0:T(8,128)(2,1)} %copy-done.1), custom_call_target="tpu_custom_call" | custom-call | tf_op jit(solution)/shard_map/collect/pallas_call | solution.py:369
  159.1 53.7 %attend.1 = bf16[256,2048]{1,0:T(8,128)(2,1)} custom-call(s32[4]{0:T(128)} %pad_add_fusion.marks, s32[1,256]{1,0:T(1,128)} %bitcast.10, s32[1,256]{1,0:T(1,128)} %fusion.hi_ref, bf16[256,2048]{1,0:T(8,128)(2,1)} %q_ref.1, bf16[4096,1024]{1,0:T(8,128)(2,1)} %bitcast.8, bf16[4096,1024]{1,0:T(8,128)(2,1)} %bitcast.9), custom_call_target="tpu_custom_call" | custom-call | tf_op jit(solution)/shard_map/attend/pallas_call | solution.py:76
Async XLA Ops:
  12.5 2.0 copy-start
  14.6 1.5 copy-start.2
  81.1 0.8 copy-start.1
